TPU v7x, 32 devices: a whole 2x2x4 slice. The times are simulated.
32 devices in a mesh: ctx: 16 (over z, y, core), tp: 2 (over x).
Axes of the slice: x: 2, y: 2, z: 4, core: 2. Of those that a mesh axis runs over, the one named last changes fastest.
Arguments:
- activations: bfloat16 [2048, 4096], P(('ctx', 'tp')), may hold values from -24 to 24
- query_weight: bfloat16 [4096, 4096], P(None, 'tp'), may hold values from -0.09375 to 0.09375
- key_weight: bfloat16 [4096, 1024], P(None, 'tp'), may hold values from -0.09375 to 0.09375
- value_weight: bfloat16 [4096, 1024], P(None, 'tp'), may hold values from -0.09375 to 0.09375
Outputs:
- attended: bfloat16 [2048, 4096], P('ctx', 'tp')
All inputs are finite; a program needn't handle non-finite values.
Results may differ from a plain program's by a relative error of at most 0.012.
The roundings to bfloat16 on the way count: a program that leaves them out, or rounds other values in their place, can miss the bound.
Values may be sent and summed in bfloat16 or wider, within the bound.
No kernel may reach another device: no remote copies, remote signals or barrier semaphores. Data moves between devices by JAX's collectives and lax.ppermute only.
A program may use at most 128 MiB of HBM per device.

v0:
```python
import math
import jax
import jax.numpy as jnp
from jax import lax
from jax.sharding import PartitionSpec as P

HD = 128
THETA = 500000.0
NEGATIVE = -1e30


def rotate(heads_in, positions):
    width = heads_in.shape[-1]
    half_width = width // 2
    frequency = THETA ** (-(jnp.arange(half_width).astype(jnp.float32) * 2.0 / width))
    angles = positions[:, None] * frequency[None, :]
    cosine = jnp.cos(angles)[:, None, :]
    sine_table = jnp.sin(angles)[:, None, :]
    front_half = heads_in[..., :half_width]
    back_half = heads_in[..., half_width:]
    return jnp.concatenate(
        [
            front_half * cosine - back_half * sine_table,
            back_half * cosine + front_half * sine_table,
        ],
        axis=-1,
    )


def block_update(state, query_block, query_pos, key_block, value_block, key_pos):
    row_top, totals, accum = state
    scale = 1.0 / math.sqrt(query_block.shape[-1])
    scores = (
        lax.dot_general(
            query_block, key_block, (((1,), (1,)), ((), ())), preferred_element_type=jnp.float32
        )
        * scale
    )
    allowed = key_pos[None, :] <= query_pos[:, None]
    block_top = jnp.max(jnp.where(allowed, scores, NEGATIVE), axis=1)
    new_top = jnp.maximum(row_top, block_top)
    correction = jnp.exp(row_top - new_top)
    weights = jnp.where(allowed, jnp.exp(scores - new_top[:, None]), 0.0)
    totals = totals * correction + jnp.sum(weights, axis=1)
    accum = accum * correction[:, None] + jnp.dot(
        weights.astype(jnp.bfloat16), value_block, preferred_element_type=jnp.float32
    )
    return (new_top, totals, accum)


def attend(groups, keys, values):
    carry_start = []
    for query_rows, query_pos, kv_slot, query_step in groups:
        row_count = query_rows.shape[0]
        blocks_count = row_count // query_step
        carry_start.append(
            (
                jnp.full((blocks_count, query_step), NEGATIVE, jnp.float32),
                jnp.zeros((blocks_count, query_step), jnp.float32),
                jnp.zeros((blocks_count, query_step, HD), jnp.float32),
            )
        )
    carry = tuple(carry_start)
    key_piece = lax.all_gather(keys, "ctx", axis=0, tiled=True)
    value_piece = lax.all_gather(values, "ctx", axis=0, tiled=True)
    piece_rows = key_piece.shape[0]
    key_step = math.gcd(piece_rows, 512)
    updated = []
    for (query_rows, query_pos, kv_slot, query_step), fold_state in zip(groups, carry):
        key_chosen = lax.dynamic_index_in_dim(
            key_piece.reshape(piece_rows, -1, HD), kv_slot, 1, keepdims=False
        )
        value_chosen = lax.dynamic_index_in_dim(
            value_piece.reshape(piece_rows, -1, HD), kv_slot, 1, keepdims=False
        )
        key_blocks = key_chosen.reshape(piece_rows // key_step, key_step, HD)
        value_blocks = value_chosen.reshape(piece_rows // key_step, key_step, HD)
        block_starts = jnp.arange(piece_rows // key_step, dtype=jnp.int32) * key_step
        blocks_count = fold_state[0].shape[0]
        query_blocks = query_rows.reshape(blocks_count, query_step, HD)
        pos_blocks = query_pos.reshape(blocks_count, query_step)

        def per_query(items):
            query_block, pos_block, row_top, totals, accum = items
            last_pos = jnp.max(pos_block)

            def per_key(inner, key_items):
                key_block, value_block, key_start = key_items
                key_pos = key_start + jnp.arange(key_step, dtype=jnp.int32)
                result = lax.cond(
                    key_start <= last_pos,
                    lambda current: block_update(
                        current, query_block, pos_block, key_block, value_block, key_pos
                    ),
                    lambda current: current,
                    inner,
                )
                return (result, None)

            final, unused = lax.scan(
                per_key, (row_top, totals, accum), (key_blocks, value_blocks, block_starts)
            )
            return final

        updated.append(
            lax.map(
                per_query, (query_blocks, pos_blocks, fold_state[0], fold_state[1], fold_state[2])
            )
        )
    final_state = tuple(updated)
    results = []
    for state in final_state:
        outcome = state[2] / state[1][..., None]
        results.append(outcome.reshape(-1, HD))
    return results


def local(activations, query_weight, key_weight, value_weight):
    tensor_count = lax.axis_size("tp")
    context_index = lax.axis_index("ctx")
    local_rows = activations.shape[0] * tensor_count
    heads_here = query_weight.shape[1] // HD
    kv_here = key_weight.shape[1] // HD
    group = heads_here // kv_here
    query_width = heads_here * HD
    key_width = kv_here * HD
    gathered = lax.all_gather(activations, "tp", axis=0, tiled=True)
    projected = jnp.concatenate(
        [
            jnp.dot(gathered, query_weight, preferred_element_type=jnp.float32),
            jnp.dot(gathered, key_weight, preferred_element_type=jnp.float32),
            jnp.dot(gathered, value_weight, preferred_element_type=jnp.float32),
        ],
        axis=1,
    )
    token_pos = context_index * local_rows + jnp.arange(local_rows, dtype=jnp.int32)
    positions = token_pos.astype(jnp.float32)
    queries = rotate(
        projected[:, :query_width].reshape(local_rows, heads_here, HD), positions
    ).astype(jnp.bfloat16)
    keys = (
        rotate(
            projected[:, query_width : query_width + key_width].reshape(local_rows, kv_here, HD),
            positions,
        )
        .astype(jnp.bfloat16)
        .reshape(local_rows, key_width)
    )
    values = projected[:, query_width + key_width :].astype(jnp.bfloat16)
    groups = []
    for kv_slot in range(kv_here):
        chosen = queries[:, kv_slot * group : (kv_slot + 1) * group].reshape(local_rows * group, HD)
        groups.append(
            (chosen, jnp.repeat(token_pos, group), kv_slot, math.gcd(local_rows * group, 512))
        )
    results = attend(groups, keys, values)
    pieces = [outcome.astype(jnp.bfloat16).reshape(local_rows, group * HD) for outcome in results]
    return jnp.concatenate(pieces, axis=1)


def solution(mesh):
    in_specs = (P(("ctx", "tp"), None), P(None, "tp"), P(None, "tp"), P(None, "tp"))
    out_specs = P("ctx", "tp")
    return jax.shard_map(local, mesh=mesh, in_specs=in_specs, out_specs=out_specs, check_vma=False)
```

profile of v0, /device:TPU:25, one launch (start us, length us, event | category | flops | bytes accessed | tf_op | source)
XLA Modules:
  0.0 219.5 jit_solution(12466268835597819170)
XLA Ops:
  7.6 23.6 %all-gather.4.cloned.1.call-done = bf16[128,4096]{1,0:T(8,128)(2,1)} async-done(((bf16[64,4096]{1,0:T(8,128)(2,1)}), bf16[128,4096]{1,0:T(8,128)(2,1)}) %all-gather.4.cloned.1.call-update) | async-done | bytes 1048592 | tf_op jit(solution)/shard_map/all_gather | solution.py:127
  31.2 3.3 %fusion.78 = f32[128,512]{1,0:T(8,128)S(1)} fusion(bf16[128,4096]{1,0:T(8,128)(2,1)} %all-gather.4.cloned.1.call-done, bf16[4096,512]{1,0:T(8,128)(2,1)} %param.22), kind=kOutput, calls=%fused_computation.123 | convolution fusion | flops 536870912 | bytes 5505024 | tf_op jit(solution)/shard_map/dot_general | solution.py:131
  36.0 3.6 %convolution_convert_fusion = bf16[128,512]{1,0:T(8,128)(2,1)} fusion(bf16[128,4096]{1,0:T(8,128)(2,1)S(1)} %copy-done, bf16[4096,512]{1,0:T(8,128)(2,1)} %param.23), kind=kOutput, calls=%fused_computation.93 | convolution fusion | flops 536936448 | bytes 5373952 | tf_op jit(solution)/shard_map/dot_general | solution.py:132
  40.3 8.2 %convolution_bitcast_fusion = f32[16,8,16,128]{3,1,2,0:T(8,128)S(1)} fusion(bf16[128,4096]{1,0:T(8,128)(2,1)S(1)} %copy-done, bf16[4096,2048]{1,0:T(8,128)(2,1)} %param.21), kind=kOutput, calls=%fused_computation.92 | convolution fusion | flops 2147483648 | bytes 18874368 | tf_op jit(solution)/shard_map/dot_general | solution.py:130
  50.6 25.6 %all-gather.6.cloned.1.call-done = bf16[2048,512]{0,1:T(8,128)(2,1)} async-done(((bf16[128,512]{0,1:T(8,128)(2,1)}), bf16[2048,512]{0,1:T(8,128)(2,1)}) %all-gather.6.cloned.1.call-update) | async-done | bytes 2097168 | tf_op jit(solution)/shard_map/all_gather | solution.py:64
  76.1 2.7 %fusion.77 = (bf16[2048,1,128]{0,2,1:T(8,128)(2,1)S(1)}, bf16[2048,1,128]{0,2,1:T(8,128)(2,1)}, bf16[2048,1,128]{0,2,1:T(8,128)(2,1)}, bf16[2048,1,128]{0,2,1:T(8,128)(2,1)}) fusion(bf16[2048,4,128]{0,2,1:T(8,128)(2,1)} %bitcast.80), kind=kLoop, calls=%fused_computation.122 | loop fusion | bytes 4194304 | tf_op jit(solution)/shard_map/jit(dynamic_index_in_dim)/dynamic_slice | solution.py:70
  79.9 39.1 %all-gather.8.cloned.1.call-done = bf16[2048,512]{1,0:T(8,128)(2,1)} async-done(((bf16[128,512]{1,0:T(8,128)(2,1)}), bf16[2048,512]{1,0:T(8,128)(2,1)}) %all-gather.8.cloned.1.call-update) | async-done | bytes 2097168 | tf_op jit(solution)/shard_map/all_gather | solution.py:65
  121.5 4.0 %fusion.76 = (bf16[2048,1,128]{2,1,0:T(2,128)(2,1)S(1)}, bf16[2048,1,128]{2,1,0:T(2,128)(2,1)}, bf16[2048,1,128]{2,1,0:T(2,128)(2,1)}, bf16[2048,1,128]{2,1,0:T(2,128)(2,1)S(1)}) fusion(bf16[2048,4,128]{2,1,0:T(4,128)(2,1)S(1)} %reshape.177), kind=kLoop, calls=%fused_computation.121 | loop fusion | bytes 4194304 | tf_op jit(solution)/shard_map/jit(dynamic_index_in_dim)/dynamic_slice | solution.py:73
  126.5 22.5 %while.96 = (s32[]{:T(128)}, f32[512]{0:T(512)S(1)}, f32[512]{0:T(512)S(1)}, f32[512,128]{1,0:T(8,128)S(1)}, s32[4]{0:T(128)S(1)}, /*index=5*/s32[]{:T(128)}, bf...) while((s32[]{:T(128)}, f32[512]{0:T(512)S(1)}, ...), condition=%wide.region_6.7_spmd.clone, body=%wide.region_1.0_spmd.clone.sunk | while | flops 137496064 | bytes 4122387 | solution.py:100
  128.3 3.8 %conditional.12 = ((f32[512]{0:T(512)S(1)}, f32[512]{0:T(512)S(1)}, f32[512,128]{1,0:T(8,128)S(1)})) conditional(s32[]{:T(128)} %convert_element_type.119, (f32[512]{0:T(512)S(1)}, f32[512]{0:T(512)S(1)}, f32[512,128]{1,0:T(8,128)S(1)}) %tuple.163, (s32[]{:T(128)}, s32[512]{0:T(512)S(1)}, s32[128]{0:T(128)S(1)}, bf16[4,512,128]{2,1,0:T(8,128)(2,1)}, ...), branch_computations={%region_2.2_spmd, %region_3.5_spmd} | conditional | flops 137496064 | bytes 4120100 | solution.py:90
  133.9 3.8 %conditional.12 = ((f32[512]{0:T(512)S(1)}, f32[512]{0:T(512)S(1)}, f32[512,128]{1,0:T(8,128)S(1)})) conditional(s32[]{:T(128)} %convert_element_type.119, (f32[512]{0:T(512)S(1)}, f32[512]{0:T(512)S(1)}, f32[512,128]{1,0:T(8,128)S(1)}) %tuple.163, (s32[]{:T(128)}, s32[512]{0:T(512)S(1)}, s32[128]{0:T(128)S(1)}, bf16[4,512,128]{2,1,0:T(8,128)(2,1)}, ...), branch_computations={%region_2.2_spmd, %region_3.5_spmd} | conditional | flops 137496064 | bytes 4120100 | solution.py:90
  139.5 3.8 %conditional.12 = ((f32[512]{0:T(512)S(1)}, f32[512]{0:T(512)S(1)}, f32[512,128]{1,0:T(8,128)S(1)})) conditional(s32[]{:T(128)} %convert_element_type.119, (f32[512]{0:T(512)S(1)}, f32[512]{0:T(512)S(1)}, f32[512,128]{1,0:T(8,128)S(1)}) %tuple.163, (s32[]{:T(128)}, s32[512]{0:T(512)S(1)}, s32[128]{0:T(128)S(1)}, bf16[4,512,128]{2,1,0:T(8,128)(2,1)}, ...), branch_computations={%region_2.2_spmd, %region_3.5_spmd} | conditional | flops 137496064 | bytes 4120100 | solution.py:90
  145.2 3.8 %conditional.12 = ((f32[512]{0:T(512)S(1)}, f32[512]{0:T(512)S(1)}, f32[512,128]{1,0:T(8,128)S(1)})) conditional(s32[]{:T(128)} %convert_element_type.119, (f32[512]{0:T(512)S(1)}, f32[512]{0:T(512)S(1)}, f32[512,128]{1,0:T(8,128)S(1)}) %tuple.163, (s32[]{:T(128)}, s32[512]{0:T(512)S(1)}, s32[128]{0:T(128)S(1)}, bf16[4,512,128]{2,1,0:T(8,128)(2,1)}, ...), branch_computations={%region_2.2_spmd, %region_3.5_spmd} | conditional | flops 137496064 | bytes 4120100 | solution.py:90
  151.2 23.1 %while.97 = (s32[]{:T(128)}, f32[512]{0:T(512)S(1)}, f32[512]{0:T(512)S(1)}, f32[512,128]{1,0:T(8,128)S(1)}, s32[4]{0:T(128)S(1)}, /*index=5*/s32[]{:T(128)}, bf...) while((s32[]{:T(128)}, f32[512]{0:T(512)S(1)}, ...), condition=%wide.region_12.13_spmd.clone, body=%wide.region_7.12_spmd.clone.sunk | while | flops 137496064 | bytes 4122387 | solution.py:100
  153.1 3.9 %conditional.13 = ((f32[512]{0:T(512)S(1)}, f32[512]{0:T(512)S(1)}, f32[512,128]{1,0:T(8,128)S(1)})) conditional(s32[]{:T(128)} %convert_element_type.120, (f32[512]{0:T(512)S(1)}, f32[512]{0:T(512)S(1)}, f32[512,128]{1,0:T(8,128)S(1)}) %tuple.166, (s32[]{:T(128)}, s32[512]{0:T(512)S(1)}, s32[128]{0:T(128)S(1)}, bf16[4,512,128]{2,1,0:T(8,128)(2,1)}, ...), branch_computations={%region_8.8_spmd, %region_9.11_spmd} | conditional | flops 137496064 | bytes 4120100 | solution.py:90
  158.9 3.9 %conditional.13 = ((f32[512]{0:T(512)S(1)}, f32[512]{0:T(512)S(1)}, f32[512,128]{1,0:T(8,128)S(1)})) conditional(s32[]{:T(128)} %convert_element_type.120, (f32[512]{0:T(512)S(1)}, f32[512]{0:T(512)S(1)}, f32[512,128]{1,0:T(8,128)S(1)}) %tuple.166, (s32[]{:T(128)}, s32[512]{0:T(512)S(1)}, s32[128]{0:T(128)S(1)}, bf16[4,512,128]{2,1,0:T(8,128)(2,1)}, ...), branch_computations={%region_8.8_spmd, %region_9.11_spmd} | conditional | flops 137496064 | bytes 4120100 | solution.py:90
  164.7 3.9 %conditional.13 = ((f32[512]{0:T(512)S(1)}, f32[512]{0:T(512)S(1)}, f32[512,128]{1,0:T(8,128)S(1)})) conditional(s32[]{:T(128)} %convert_element_type.120, (f32[512]{0:T(512)S(1)}, f32[512]{0:T(512)S(1)}, f32[512,128]{1,0:T(8,128)S(1)}) %tuple.166, (s32[]{:T(128)}, s32[512]{0:T(512)S(1)}, s32[128]{0:T(128)S(1)}, bf16[4,512,128]{2,1,0:T(8,128)(2,1)}, ...), branch_computations={%region_8.8_spmd, %region_9.11_spmd} | conditional | flops 137496064 | bytes 4120100 | solution.py:90
  170.4 3.9 %conditional.13 = ((f32[512]{0:T(512)S(1)}, f32[512]{0:T(512)S(1)}, f32[512,128]{1,0:T(8,128)S(1)})) conditional(s32[]{:T(128)} %convert_element_type.120, (f32[512]{0:T(512)S(1)}, f32[512]{0:T(512)S(1)}, f32[512,128]{1,0:T(8,128)S(1)}) %tuple.166, (s32[]{:T(128)}, s32[512]{0:T(512)S(1)}, s32[128]{0:T(128)S(1)}, bf16[4,512,128]{2,1,0:T(8,128)(2,1)}, ...), branch_computations={%region_8.8_spmd, %region_9.11_spmd} | conditional | flops 137496064 | bytes 4120100 | solution.py:90
  175.7 19.9 %while.98 = (s32[]{:T(128)}, f32[512]{0:T(512)S(1)}, f32[512]{0:T(512)S(1)}, f32[512,128]{1,0:T(8,128)S(1)}, s32[4]{0:T(128)S(1)}, /*index=5*/s32[]{:T(128)}, bf...) while((s32[]{:T(128)}, f32[512]{0:T(512)S(1)}, ...), condition=%wide.region_18.19_spmd.clone, body=%wide.region_13.18_spmd.clone.sunk | while | flops 137496064 | bytes 4121879 | solution.py:100
  177.8 2.9 %conditional.14 = ((f32[512]{0:T(512)S(1)}, f32[512]{0:T(512)S(1)}, f32[512,128]{1,0:T(8,128)S(1)})) conditional(s32[]{:T(128)} %convert_element_type.121, (f32[512]{0:T(512)S(1)}, f32[512]{0:T(512)S(1)}, f32[512,128]{1,0:T(8,128)S(1)}) %tuple.169, (s32[]{:T(128)}, s32[512]{0:T(512)S(1)}, s32[128]{0:T(128)S(1)}, bf16[4,512,128]{2,1,0:T(8,128)(2,1)}, ...), branch_computations={%region_14.14_spmd, %region_15.17_spmd} | conditional | flops 137496064 | bytes 4119592 | solution.py:90
  182.7 2.9 %conditional.14 = ((f32[512]{0:T(512)S(1)}, f32[512]{0:T(512)S(1)}, f32[512,128]{1,0:T(8,128)S(1)})) conditional(s32[]{:T(128)} %convert_element_type.121, (f32[512]{0:T(512)S(1)}, f32[512]{0:T(512)S(1)}, f32[512,128]{1,0:T(8,128)S(1)}) %tuple.169, (s32[]{:T(128)}, s32[512]{0:T(512)S(1)}, s32[128]{0:T(128)S(1)}, bf16[4,512,128]{2,1,0:T(8,128)(2,1)}, ...), branch_computations={%region_14.14_spmd, %region_15.17_spmd} | conditional | flops 137496064 | bytes 4119592 | solution.py:90
  187.7 2.9 %conditional.14 = ((f32[512]{0:T(512)S(1)}, f32[512]{0:T(512)S(1)}, f32[512,128]{1,0:T(8,128)S(1)})) conditional(s32[]{:T(128)} %convert_element_type.121, (f32[512]{0:T(512)S(1)}, f32[512]{0:T(512)S(1)}, f32[512,128]{1,0:T(8,128)S(1)}) %tuple.169, (s32[]{:T(128)}, s32[512]{0:T(512)S(1)}, s32[128]{0:T(128)S(1)}, bf16[4,512,128]{2,1,0:T(8,128)(2,1)}, ...), branch_computations={%region_14.14_spmd, %region_15.17_spmd} | conditional | flops 137496064 | bytes 4119592 | solution.py:90
  192.7 2.9 %conditional.14 = ((f32[512]{0:T(512)S(1)}, f32[512]{0:T(512)S(1)}, f32[512,128]{1,0:T(8,128)S(1)})) conditional(s32[]{:T(128)} %convert_element_type.121, (f32[512]{0:T(512)S(1)}, f32[512]{0:T(512)S(1)}, f32[512,128]{1,0:T(8,128)S(1)}) %tuple.169, (s32[]{:T(128)}, s32[512]{0:T(512)S(1)}, s32[128]{0:T(128)S(1)}, bf16[4,512,128]{2,1,0:T(8,128)(2,1)}, ...), branch_computations={%region_14.14_spmd, %region_15.17_spmd} | conditional | flops 137496064 | bytes 4119592 | solution.py:90
  196.3 15.6 %while.99 = (s32[]{:T(128)}, f32[512]{0:T(512)S(1)}, f32[512]{0:T(512)S(1)}, f32[512,128]{1,0:T(8,128)S(1)}, s32[4]{0:T(128)S(1)}, /*index=5*/s32[]{:T(128)}, bf...) while((s32[]{:T(128)}, f32[512]{0:T(512)S(1)}, ...), condition=%wide.region_24.25_spmd.clone, body=%wide.region_19.24_spmd.clone.sunk | while | flops 137496064 | bytes 4121371 | solution.py:100
  (240 shorter events, 82.3 us)
Async XLA Ops:
  6.5 24.7 %all-gather.4.cloned.1.call-start = ((), (), s32[]{:S(2)}) async-start(), calls=%async_computation | async-start | bytes 1572864 | tf_op jit(solution)/shard_map/all_gather | solution.py:127
  7.3 68.9 %all-gather.6.cloned.1.call-start = ((), (), s32[]{:S(2)}) async-start(), calls=%async_computation.1 | async-start | bytes 2228224 | tf_op jit(solution)/shard_map/all_gather | solution.py:64
  31.2 4.8 %copy-start = (bf16[128,4096]{1,0:T(8,128)(2,1)S(1)}, bf16[128,4096]{1,0:T(8,128)(2,1)}, u32[]{:S(2)}) copy-start(bf16[128,4096]{1,0:T(8,128)(2,1)} %all-gather.4.cloned.1.call-done) | copy-start | bytes 3145732
  35.9 83.1 %all-gather.8.cloned.1.call-start = ((), (), s32[]{:S(2)}) async-start(), calls=%async_computation.2 | async-start | bytes 2228224 | tf_op jit(solution)/shard_map/all_gather | solution.py:65
  126.5 22.7 %copy-start.5 = (bf16[2048,1,128]{0,2,1:T(8,128)(2,1)S(1)}, bf16[2048,1,128]{0,2,1:T(8,128)(2,1)}, u32[]{:S(2)}) copy-start(bf16[2048,1,128]{0,2,1:T(8,128)(2,1)} %get-tuple-element.984) | copy-start | bytes 1572868
  126.5 23.7 %copy-start.2 = (bf16[2048,1,128]{2,1,0:T(2,128)(2,1)S(1)}, bf16[2048,1,128]{2,1,0:T(2,128)(2,1)}, u32[]{:S(2)}) copy-start(bf16[2048,1,128]{2,1,0:T(2,128)(2,1)} %get-tuple-element.979) | copy-start | bytes 1572868
  151.2 23.4 %copy-start.4 = (bf16[2048,1,128]{0,2,1:T(8,128)(2,1)S(1)}, bf16[2048,1,128]{0,2,1:T(8,128)(2,1)}, u32[]{:S(2)}) copy-start(bf16[2048,1,128]{0,2,1:T(8,128)(2,1)} %get-tuple-element.983) | copy-start | bytes 1572868
  151.2 24.4 %copy-start.1 = (bf16[2048,1,128]{2,1,0:T(2,128)(2,1)S(1)}, bf16[2048,1,128]{2,1,0:T(2,128)(2,1)}, u32[]{:S(2)}) copy-start(bf16[2048,1,128]{2,1,0:T(2,128)(2,1)} %get-tuple-element.978) | copy-start | bytes 1572868
  175.7 20.1 %copy-start.3 = (bf16[2048,1,128]{0,2,1:T(8,128)(2,1)S(1)}, bf16[2048,1,128]{0,2,1:T(8,128)(2,1)}, u32[]{:S(2)}) copy-start(bf16[2048,1,128]{0,2,1:T(8,128)(2,1)} %get-tuple-element.982) | copy-start | bytes 1572868
Sparse Core Ops, SparseCore 0:
  8.9 22.2 all-gather.3
  36.0 40.0 all-gather.5
  78.3 40.6 all-gather.7
where the time goes:
time: 221 us; the launch traced here: 219 us
  waiting for transfers between devices  89 us (40%)
  matrix products  47.3 us (21%)
  local copies, waits for them, and re-layouts  28.9 us (13%)
  loops' own time  21.6 us (10%)
  other arithmetic  19.1 us (9%)
  between operations  13.5 us (6%)
    all_gather x1, waiting for transfers between devices, attend(): value_piece = lax.all_gather(values, 'ctx', axis=0, tiled=True)  39.1 us
    all_gather x1, waiting for transfers between devices, attend(): key_piece = lax.all_gather(keys, 'ctx', axis=0, tiled=True)  25.6 us
    all_gather x1, waiting for transfers between devices, local(): gathered = lax.all_gather(activations, 'tp', axis=0, tiled=True)  23.6 us
    another operation x4, loops' own time, per_query(): lax.scan(per_key, (row_top, totals, accum), (key_blocks, value_blocks, bl...  20.8 us
    dot_general x16, matrix products, block_update(): lax.dot_general(query_block, key_block, (((1,), (1,)), ((), ())), preferr...  16.5 us
    dot_general x16, matrix products, block_update(): jnp.dot(weights.astype(jnp.bfloat16), value_block, preferred_element_type...  15.7 us
    add x16, other arithmetic, per_key(): key_pos = key_start + jnp.arange(key_step, dtype=jnp.int32)  10.2 us
    dynamic_slice x16, local copies, waits for them, and re-layouts, per_query(): lax.scan(per_key, (row_top, totals, accum), (key_blocks, value_blocks, bl...  9.76 us
  transfers between devices with their start and end apart: 3, of which 3 were waited for; matrix products, arithmetic and copies ran while one was open for 8% of the time, Pallas kernels for 0%

commit v1 on v0

--- a/solution.py
+++ b/solution.py
@@ -3,10 +3,17 @@
 import jax.numpy as jnp
 from jax import lax
 from jax.sharding import PartitionSpec as P
+from jax.lax import axis_index, axis_size, ppermute
 
 HD = 128
 THETA = 500000.0
 NEGATIVE = -1e30
+
+
+def links_settle(body, dim_at):
+    finding = list(body.shape[1:])
+    finding[dim_at] *= body.shape[0]
+    return jnp.moveaxis(body, 0, dim_at).reshape(finding)
 
 
 def rotate(heads_in, positions):
@@ -61,7 +68,21 @@
             )
         )
     carry = tuple(carry_start)
-    key_piece = lax.all_gather(keys, "ctx", axis=0, tiled=True)
+    lanes = axis_size("ctx")
+    history = [(w, (w + 1) % lanes) for w in range(lanes)]
+    samples = [(h, dev_i) for dev_i, h in history]
+    small, spare = ([], [])
+    for dd in range(lanes - 1):
+        if dd % 2 == 0:
+            new = ppermute(small[-1] if small else keys, "ctx", history)
+            small.append(new)
+        else:
+            spare.append(ppermute(spare[-1] if spare else keys, "ctx", samples))
+    mid_arr = jnp.stack([*small[::-1], keys, *spare])
+    arr_out = axis_index("ctx")
+    extra = arr_out - len(small)
+    mid_arr = mid_arr[(jnp.arange(lanes) - extra) % lanes]
+    key_piece = links_settle(mid_arr, 0)
     value_piece = lax.all_gather(values, "ctx", axis=0, tiled=True)
     piece_rows = key_piece.shape[0]
     key_step = math.gcd(piece_rows, 512)

time: 221 us -> 207 us (0.937)
  waiting for transfers between devices: 89 us -> 53.5 us
  starting transfers between devices: 0.08 us -> 26.5 us
  matrix products: 47.3 us -> 43.1 us
  local copies, waits for them, and re-layouts: 28.9 us -> 31.3 us
    all_gather x1, waiting for transfers between devices: 39.1 us -> 10.6 us  [attend(): value_piece = lax.all_gather(values, 'ctx', axis=0, tiled=True)]
    ppermute x0 -> x15, starting transfers between devices: none -> 26.4 us  [the longest x8 25.5 us: attend(): new = ppermute(small[-1] if small else keys, 'ctx', history)]
    all_gather x1 -> x0, waiting for transfers between devices: 25.6 us -> none  [attend(): key_piece = lax.all_gather(keys, 'ctx', axis=0, tiled=True)]
    ppermute x0 -> x15, waiting for transfers between devices: none -> 18.6 us  [the longest x7 13.7 us: attend(): spare.append(ppermute(spare[-1] if spare else keys, 'ctx', samples))]
    dot_general x16, matrix products: 15.7 us -> 8.29 us  [block_update(): jnp.dot(weights.astype(jnp.bfloat16), value_block, preferred_element_type...]
    dot_general x16, matrix products: 16.5 us -> 19.9 us  [block_update(): lax.dot_general(query_block, key_block, (((1,), (1,)), ((), ())), preferr...]
    another operation x0 -> x2, local copies, waits for them, and re-layouts: none -> 2.55 us  [the longest x1 2.55 us: attend(): key_piece.reshape(piece_rows, -1, HD)]
    unnamed x21 -> x43, local copies, waits for them, and re-layouts: 5.44 us -> 4.15 us
  transfers between devices with their start and end apart: 3 -> 17, of which waited for: 3 -> 12; matrix products, arithmetic and copies ran while one was open for 8% -> 13% of each run, Pallas kernels for 0% -> 0%
where the time goes in v1:
time: 207 us; the launch traced here: 206 us
  waiting for transfers between devices  53.5 us (26%)
  matrix products  43.1 us (21%)
  local copies, waits for them, and re-layouts  31.3 us (15%)
  starting transfers between devices  26.5 us (13%)
  loops' own time  19.7 us (10%)
  other arithmetic  18 us (9%)
  between operations  14 us (7%)
    ppermute x8, starting transfers between devices, attend(): new = ppermute(small[-1] if small else keys, 'ctx', history)  25.5 us
    all_gather x1, waiting for transfers between devices, local(): gathered = lax.all_gather(activations, 'tp', axis=0, tiled=True)  23.6 us
    dot_general x16, matrix products, block_update(): lax.dot_general(query_block, key_block, (((1,), (1,)), ((), ())), preferr...  19.9 us
    another operation x4, loops' own time, per_query(): lax.scan(per_key, (row_top, totals, accum), (key_blocks, value_blocks, bl...  18.8 us
    ppermute x7, waiting for transfers between devices, attend(): spare.append(ppermute(spare[-1] if spare else keys, 'ctx', samples))  13.7 us
    all_gather x1, waiting for transfers between devices, attend(): value_piece = lax.all_gather(values, 'ctx', axis=0, tiled=True)  10.6 us
    dynamic_slice x16, local copies, waits for them, and re-layouts, per_query(): lax.scan(per_key, (row_top, totals, accum), (key_blocks, value_blocks, bl...  9.26 us
    add x16, other arithmetic, per_key(): key_pos = key_start + jnp.arange(key_step, dtype=jnp.int32)  9.23 us
  transfers between devices with their start and end apart: 17, of which 12 were waited for; matrix products, arithmetic and copies ran while one was open for 13% of the time, Pallas kernels for 0%

profile of v1, /device:TPU:25, one launch (start us, length us, event | category | flops | bytes accessed | tf_op | source)
XLA Modules:
  0.0 206.0 jit_solution(9543712272757769611)
XLA Ops:
  7.6 23.6 %all-gather.3.cloned.1.call-done = bf16[128,4096]{1,0:T(8,128)(2,1)} async-done(((bf16[64,4096]{1,0:T(8,128)(2,1)}), bf16[128,4096]{1,0:T(8,128)(2,1)}) %all-gather.3.cloned.1.call-update) | async-done | bytes 1048592 | tf_op jit(solution)/shard_map/all_gather | solution.py:148
  31.2 3.2 %fusion.80 = f32[128,512]{1,0:T(8,128)S(1)} fusion(bf16[128,4096]{1,0:T(8,128)(2,1)} %all-gather.3.cloned.1.call-done, bf16[4096,512]{1,0:T(8,128)(2,1)} %param.22), kind=kOutput, calls=%fused_computation.148 | convolution fusion | flops 536870912 | bytes 5505024 | tf_op jit(solution)/shard_map/dot_general | solution.py:152
  54.7 3.2 %collective-permute-done.10 = bf16[128,512]{1,0:T(8,128)(2,1)S(1)} collective-permute-done((bf16[128,512]{1,0:T(8,128)(2,1)S(1)}, bf16[128,512]{1,0:T(8,128)(2,1)S(1)}, u32[]{:S(2)}, u32[]{:S(2)}) %collective-permute-start.10) | collective-permute-done | bytes 131104 | tf_op jit(solution)/shard_map/ppermute | solution.py:80
  58.1 3.7 %collective-permute-start.5 = (bf16[128,512]{1,0:T(8,128)(2,1)S(1)}, bf16[128,512]{1,0:T(8,128)(2,1)S(1)}, u32[]{:S(2)}, u32[]{:S(2)}) collective-permute-start(bf16[128,512]{1,0:T(8,128)(2,1)S(1)} %collective-permute-done.4), channel_id=1, source_target_pairs={{0,2},{2,4},{4,6},{6,8},{8,10},{10,12},{12,14},{14,16},{16,18},{18... | collective-permute-start | bytes 393224 | tf_op jit(solution)/shard_map/ppermute | solution.py:77
  61.9 3.6 %convolution_convert_fusion = bf16[128,512]{1,0:T(8,128)(2,1)} fusion(bf16[128,4096]{1,0:T(8,128)(2,1)S(1)} %copy-done, bf16[4096,512]{1,0:T(8,128)(2,1)} %param.23), kind=kOutput, calls=%fused_computation.94 | convolution fusion | flops 536936448 | bytes 5373952 | tf_op jit(solution)/shard_map/dot_general | solution.py:153
  66.4 5.5 %collective-permute-start.6 = (bf16[128,512]{1,0:T(8,128)(2,1)S(1)}, bf16[128,512]{1,0:T(8,128)(2,1)S(1)}, u32[]{:S(2)}, u32[]{:S(2)}) collective-permute-start(bf16[128,512]{1,0:T(8,128)(2,1)S(1)} %collective-permute-done.5), channel_id=1, source_target_pairs={{0,2},{2,4},{4,6},{6,8},{8,10},{10,12},{12,14},{14,16},{16,18},{18... | collective-permute-start | bytes 393224 | tf_op jit(solution)/shard_map/ppermute | solution.py:77
  71.9 8.1 %convolution_bitcast_fusion = f32[16,8,16,128]{3,1,2,0:T(8,128)S(1)} fusion(bf16[128,4096]{1,0:T(8,128)(2,1)S(1)} %copy-done, bf16[4096,2048]{1,0:T(8,128)(2,1)} %param.21), kind=kOutput, calls=%fused_computation.93 | convolution fusion | flops 2147483648 | bytes 18874368 | tf_op jit(solution)/shard_map/dot_general | solution.py:151
  80.3 5.2 %collective-permute-start.7 = (bf16[128,512]{1,0:T(8,128)(2,1)S(1)}, bf16[128,512]{1,0:T(8,128)(2,1)S(1)}, u32[]{:S(2)}, u32[]{:S(2)}) collective-permute-start(bf16[128,512]{1,0:T(8,128)(2,1)S(1)} %collective-permute-done.6), channel_id=1, source_target_pairs={{0,2},{2,4},{4,6},{6,8},{8,10},{10,12},{12,14},{14,16},{16,18},{18... | collective-permute-start | bytes 393224 | tf_op jit(solution)/shard_map/ppermute | solution.py:77
  88.6 6.2 %collective-permute-done.14 = bf16[128,512]{1,0:T(8,128)(2,1)S(1)} collective-permute-done((bf16[128,512]{1,0:T(8,128)(2,1)S(1)}, bf16[128,512]{1,0:T(8,128)(2,1)S(1)}, u32[]{:S(2)}, u32[]{:S(2)}) %collective-permute-start.14) | collective-permute-done | bytes 131104 | tf_op jit(solution)/shard_map/ppermute | solution.py:80
  99.4 3.1 %fusion.79 = (bf16[2048,1,128]{2,1,0:T(2,128)(2,1)S(1)}, bf16[2048,1,128]{2,1,0:T(2,128)(2,1)S(1)}, bf16[2048,1,128]{2,1,0:T(2,128)(2,1)S(1)}, bf16[2048,1,128]{2,1,0:T(2,128)(2,1)S(1)}) fusion(bf16[2048,4,128]{2,1,0:T(4,128)(2,1)S(1)} %reshape.246), kind=kLoop, calls=%fused_computation.147 | loop fusion | bytes 4194304 | tf_op jit(solution)/shard_map/jit(dynamic_index_in_dim)/dynamic_slice | solution.py:91
  105.9 10.6 %all-gather.5.cloned.1.call-done = bf16[2048,512]{1,0:T(8,128)(2,1)} async-done(((bf16[128,512]{1,0:T(8,128)(2,1)}), bf16[2048,512]{1,0:T(8,128)(2,1)}) %all-gather.5.cloned.1.call-update) | async-done | bytes 2097168 | tf_op jit(solution)/shard_map/all_gather | solution.py:86
  119.1 4.0 %fusion.78 = (bf16[2048,1,128]{2,1,0:T(2,128)(2,1)S(1)}, bf16[2048,1,128]{2,1,0:T(2,128)(2,1)}, bf16[2048,1,128]{2,1,0:T(2,128)(2,1)}, bf16[2048,1,128]{2,1,0:T(2,128)(2,1)S(1)}) fusion(bf16[2048,4,128]{2,1,0:T(4,128)(2,1)S(1)} %reshape.230), kind=kLoop, calls=%fused_computation.146 | loop fusion | bytes 4194304 | tf_op jit(solution)/shard_map/jit(dynamic_index_in_dim)/dynamic_slice | solution.py:94
  123.3 18.2 %while.96 = (s32[]{:T(128)}, f32[512]{0:T(512)S(1)}, f32[512]{0:T(512)S(1)}, f32[512,128]{1,0:T(8,128)S(1)}, s32[4]{0:T(128)S(1)}, /*index=5*/s32[]{:T(128)}, bf...) while((s32[]{:T(128)}, f32[512]{0:T(512)S(1)}, ...), condition=%wide.region_6.7_spmd.clone, body=%wide.region_1.6_spmd.clone.sunk | while | flops 137496064 | bytes 4121887 | solution.py:121
  125.0 2.9 %conditional.12 = ((f32[512]{0:T(512)S(1)}, f32[512]{0:T(512)S(1)}, f32[512,128]{1,0:T(8,128)S(1)})) conditional(s32[]{:T(128)} %convert_element_type.134, (f32[512]{0:T(512)S(1)}, f32[512]{0:T(512)S(1)}, f32[512,128]{1,0:T(8,128)S(1)}) %tuple.167, (s32[]{:T(128)}, s32[512]{0:T(512)S(1)}, s32[128]{0:T(128)S(1)}, bf16[4,512,128]{2,1,0:T(8,128)(2,1)}, ...), branch_computations={%region_2.2_spmd, %region_3.5_spmd} | conditional | flops 137496064 | bytes 4119592 | solution.py:111
  129.5 2.9 %conditional.12 = ((f32[512]{0:T(512)S(1)}, f32[512]{0:T(512)S(1)}, f32[512,128]{1,0:T(8,128)S(1)})) conditional(s32[]{:T(128)} %convert_element_type.134, (f32[512]{0:T(512)S(1)}, f32[512]{0:T(512)S(1)}, f32[512,128]{1,0:T(8,128)S(1)}) %tuple.167, (s32[]{:T(128)}, s32[512]{0:T(512)S(1)}, s32[128]{0:T(128)S(1)}, bf16[4,512,128]{2,1,0:T(8,128)(2,1)}, ...), branch_computations={%region_2.2_spmd, %region_3.5_spmd} | conditional | flops 137496064 | bytes 4119592 | solution.py:111
  134.1 2.9 %conditional.12 = ((f32[512]{0:T(512)S(1)}, f32[512]{0:T(512)S(1)}, f32[512,128]{1,0:T(8,128)S(1)})) conditional(s32[]{:T(128)} %convert_element_type.134, (f32[512]{0:T(512)S(1)}, f32[512]{0:T(512)S(1)}, f32[512,128]{1,0:T(8,128)S(1)}) %tuple.167, (s32[]{:T(128)}, s32[512]{0:T(512)S(1)}, s32[128]{0:T(128)S(1)}, bf16[4,512,128]{2,1,0:T(8,128)(2,1)}, ...), branch_computations={%region_2.2_spmd, %region_3.5_spmd} | conditional | flops 137496064 | bytes 4119592 | solution.py:111
  138.7 2.9 %conditional.12 = ((f32[512]{0:T(512)S(1)}, f32[512]{0:T(512)S(1)}, f32[512,128]{1,0:T(8,128)S(1)})) conditional(s32[]{:T(128)} %convert_element_type.134, (f32[512]{0:T(512)S(1)}, f32[512]{0:T(512)S(1)}, f32[512,128]{1,0:T(8,128)S(1)}) %tuple.167, (s32[]{:T(128)}, s32[512]{0:T(512)S(1)}, s32[128]{0:T(128)S(1)}, bf16[4,512,128]{2,1,0:T(8,128)(2,1)}, ...), branch_computations={%region_2.2_spmd, %region_3.5_spmd} | conditional | flops 137496064 | bytes 4119592 | solution.py:111
  141.9 18.3 %while.98 = (s32[]{:T(128)}, f32[512]{0:T(512)S(1)}, f32[512]{0:T(512)S(1)}, f32[512,128]{1,0:T(8,128)S(1)}, s32[4]{0:T(128)S(1)}, /*index=5*/s32[]{:T(128)}, bf...) while((s32[]{:T(128)}, f32[512]{0:T(512)S(1)}, ...), condition=%wide.region_18.19_spmd.clone, body=%wide.region_13.18_spmd.clone.sunk | while | flops 137496064 | bytes 4121887 | solution.py:121
  160.6 18.7 %while.97 = (s32[]{:T(128)}, f32[512]{0:T(512)S(1)}, f32[512]{0:T(512)S(1)}, f32[512,128]{1,0:T(8,128)S(1)}, s32[4]{0:T(128)S(1)}, /*index=5*/s32[]{:T(128)}, bf...) while((s32[]{:T(128)}, f32[512]{0:T(512)S(1)}, ...), condition=%wide.region_12.13_spmd.clone, body=%wide.region_7.12_spmd.clone.sunk | while | flops 137496064 | bytes 4121887 | solution.py:121
  162.4 2.9 %conditional.13 = ((f32[512]{0:T(512)S(1)}, f32[512]{0:T(512)S(1)}, f32[512,128]{1,0:T(8,128)S(1)})) conditional(s32[]{:T(128)} %convert_element_type.135, (f32[512]{0:T(512)S(1)}, f32[512]{0:T(512)S(1)}, f32[512,128]{1,0:T(8,128)S(1)}) %tuple.170, (s32[]{:T(128)}, s32[512]{0:T(512)S(1)}, s32[128]{0:T(128)S(1)}, bf16[4,512,128]{2,1,0:T(8,128)(2,1)}, ...), branch_computations={%region_8.8_spmd, %region_9.11_spmd} | conditional | flops 137496064 | bytes 4119592 | solution.py:111
  167.1 2.9 %conditional.13 = ((f32[512]{0:T(512)S(1)}, f32[512]{0:T(512)S(1)}, f32[512,128]{1,0:T(8,128)S(1)})) conditional(s32[]{:T(128)} %convert_element_type.135, (f32[512]{0:T(512)S(1)}, f32[512]{0:T(512)S(1)}, f32[512,128]{1,0:T(8,128)S(1)}) %tuple.170, (s32[]{:T(128)}, s32[512]{0:T(512)S(1)}, s32[128]{0:T(128)S(1)}, bf16[4,512,128]{2,1,0:T(8,128)(2,1)}, ...), branch_computations={%region_8.8_spmd, %region_9.11_spmd} | conditional | flops 137496064 | bytes 4119592 | solution.py:111
  171.8 2.9 %conditional.13 = ((f32[512]{0:T(512)S(1)}, f32[512]{0:T(512)S(1)}, f32[512,128]{1,0:T(8,128)S(1)})) conditional(s32[]{:T(128)} %convert_element_type.135, (f32[512]{0:T(512)S(1)}, f32[512]{0:T(512)S(1)}, f32[512,128]{1,0:T(8,128)S(1)}) %tuple.170, (s32[]{:T(128)}, s32[512]{0:T(512)S(1)}, s32[128]{0:T(128)S(1)}, bf16[4,512,128]{2,1,0:T(8,128)(2,1)}, ...), branch_computations={%region_8.8_spmd, %region_9.11_spmd} | conditional | flops 137496064 | bytes 4119592 | solution.py:111
  176.4 2.9 %conditional.13 = ((f32[512]{0:T(512)S(1)}, f32[512]{0:T(512)S(1)}, f32[512,128]{1,0:T(8,128)S(1)})) conditional(s32[]{:T(128)} %convert_element_type.135, (f32[512]{0:T(512)S(1)}, f32[512]{0:T(512)S(1)}, f32[512,128]{1,0:T(8,128)S(1)}) %tuple.170, (s32[]{:T(128)}, s32[512]{0:T(512)S(1)}, s32[128]{0:T(128)S(1)}, bf16[4,512,128]{2,1,0:T(8,128)(2,1)}, ...), branch_computations={%region_8.8_spmd, %region_9.11_spmd} | conditional | flops 137496064 | bytes 4119592 | solution.py:111
  179.7 18.4 %while.99 = (s32[]{:T(128)}, f32[512]{0:T(512)S(1)}, f32[512]{0:T(512)S(1)}, f32[512,128]{1,0:T(8,128)S(1)}, s32[4]{0:T(128)S(1)}, /*index=5*/s32[]{:T(128)}, bf...) while((s32[]{:T(128)}, f32[512]{0:T(512)S(1)}, ...), condition=%wide.region_24.25_spmd.clone, body=%wide.region_19.24_spmd.clone.sunk | while | flops 137496064 | bytes 4121887 | solution.py:121
  (294 shorter events, 114.8 us)
Async XLA Ops:
  6.5 24.7 %all-gather.3.cloned.1.call-start = ((), (), s32[]{:S(2)}) async-start(), calls=%async_computation | async-start | bytes 1572864 | tf_op jit(solution)/shard_map/all_gather | solution.py:148
  7.3 109.3 %all-gather.5.cloned.1.call-start = ((), (), s32[]{:S(2)}) async-start(), calls=%async_computation.1 | async-start | bytes 2228224 | tf_op jit(solution)/shard_map/all_gather | solution.py:86
  34.4 27.4 %copy-start = (bf16[128,4096]{1,0:T(8,128)(2,1)S(1)}, bf16[128,4096]{1,0:T(8,128)(2,1)}, u32[]{:S(2)}) copy-start(bf16[128,4096]{1,0:T(8,128)(2,1)} %all-gather.3.cloned.1.call-done) | copy-start | bytes 3145732
  35.1 3.8 %collective-permute-start = (bf16[128,512]{1,0:T(8,128)(2,1)S(1)}, bf16[128,512]{1,0:T(8,128)(2,1)S(1)}, u32[]{:S(2)}, u32[]{:S(2)}) collective-permute-start(bf16[128,512]{1,0:T(8,128)(2,1)S(1)} %bitcast.127), channel_id=1, source_target_pairs={{0,2},{2,4},{4,6},{6,8},{8,10},{10,12},{12,14},{14,16},{16,18},{18... | collective-permute-start | bytes 393224 | tf_op jit(solution)/shard_map/ppermute | solution.py:77
  38.8 4.4 %collective-permute-start.1 = (bf16[128,512]{1,0:T(8,128)(2,1)S(1)}, bf16[128,512]{1,0:T(8,128)(2,1)S(1)}, u32[]{:S(2)}, u32[]{:S(2)}) collective-permute-start(bf16[128,512]{1,0:T(8,128)(2,1)S(1)} %collective-permute-done), channel_id=1, source_target_pairs={{0,2},{2,4},{4,6},{6,8},{8,10},{10,12},{12,14},{14,16},{16,18},{18... | collective-permute-start | bytes 393224 | tf_op jit(solution)/shard_map/ppermute | solution.py:77
  41.3 5.8 %collective-permute-start.8 = (bf16[128,512]{1,0:T(8,128)(2,1)S(1)}, bf16[128,512]{1,0:T(8,128)(2,1)S(1)}, u32[]{:S(2)}, u32[]{:S(2)}) collective-permute-start(bf16[128,512]{1,0:T(8,128)(2,1)S(1)} %bitcast.128), channel_id=1, source_target_pairs={{2,0},{4,2},{6,4},{8,6},{10,8},{12,10},{14,12},{16,14},{18,16},{20... | collective-permute-start | bytes 393224 | tf_op jit(solution)/shard_map/ppermute | solution.py:80
  43.2 4.4 %collective-permute-start.2 = (bf16[128,512]{1,0:T(8,128)(2,1)S(1)}, bf16[128,512]{1,0:T(8,128)(2,1)S(1)}, u32[]{:S(2)}, u32[]{:S(2)}) collective-permute-start(bf16[128,512]{1,0:T(8,128)(2,1)S(1)} %collective-permute-done.1), channel_id=1, source_target_pairs={{0,2},{2,4},{4,6},{6,8},{8,10},{10,12},{12,14},{14,16},{16,18},{18... | collective-permute-start | bytes 393224 | tf_op jit(solution)/shard_map/ppermute | solution.py:77
  47.1 5.4 %collective-permute-start.9 = (bf16[128,512]{1,0:T(8,128)(2,1)S(1)}, bf16[128,512]{1,0:T(8,128)(2,1)S(1)}, u32[]{:S(2)}, u32[]{:S(2)}) collective-permute-start(bf16[128,512]{1,0:T(8,128)(2,1)S(1)} %collective-permute-done.8), channel_id=1, source_target_pairs={{2,0},{4,2},{6,4},{8,6},{10,8},{12,10},{14,12},{16,14},{18,16},{20... | collective-permute-start | bytes 393224 | tf_op jit(solution)/shard_map/ppermute | solution.py:80
  47.6 5.1 %collective-permute-start.3 = (bf16[128,512]{1,0:T(8,128)(2,1)S(1)}, bf16[128,512]{1,0:T(8,128)(2,1)S(1)}, u32[]{:S(2)}, u32[]{:S(2)}) collective-permute-start(bf16[128,512]{1,0:T(8,128)(2,1)S(1)} %collective-permute-done.2), channel_id=1, source_target_pairs={{0,2},{2,4},{4,6},{6,8},{8,10},{10,12},{12,14},{14,16},{16,18},{18... | collective-permute-start | bytes 393224 | tf_op jit(solution)/shard_map/ppermute | solution.py:77
  52.5 5.4 %collective-permute-start.10 = (bf16[128,512]{1,0:T(8,128)(2,1)S(1)}, bf16[128,512]{1,0:T(8,128)(2,1)S(1)}, u32[]{:S(2)}, u32[]{:S(2)}) collective-permute-start(bf16[128,512]{1,0:T(8,128)(2,1)S(1)} %collective-permute-done.9), channel_id=1, source_target_pairs={{2,0},{4,2},{6,4},{8,6},{10,8},{12,10},{14,12},{16,14},{18,16},{20... | collective-permute-start | bytes 393224 | tf_op jit(solution)/shard_map/ppermute | solution.py:80
  52.7 5.4 %collective-permute-start.4 = (bf16[128,512]{1,0:T(8,128)(2,1)S(1)}, bf16[128,512]{1,0:T(8,128)(2,1)S(1)}, u32[]{:S(2)}, u32[]{:S(2)}) collective-permute-start(bf16[128,512]{1,0:T(8,128)(2,1)S(1)} %collective-permute-done.3), channel_id=1, source_target_pairs={{0,2},{2,4},{4,6},{6,8},{8,10},{10,12},{12,14},{14,16},{16,18},{18... | collective-permute-start | bytes 393224 | tf_op jit(solution)/shard_map/ppermute | solution.py:77
  57.9 7.6 %collective-permute-start.11 = (bf16[128,512]{1,0:T(8,128)(2,1)S(1)}, bf16[128,512]{1,0:T(8,128)(2,1)S(1)}, u32[]{:S(2)}, u32[]{:S(2)}) collective-permute-start(bf16[128,512]{1,0:T(8,128)(2,1)S(1)} %collective-permute-done.10), channel_id=1, source_target_pairs={{2,0},{4,2},{6,4},{8,6},{10,8},{12,10},{14,12},{16,14},{18,16},{20... | collective-permute-start | bytes 393224 | tf_op jit(solution)/shard_map/ppermute | solution.py:80
  58.1 7.3 %copy-start.5 = (bf16[128,512]{1,0:T(8,128)(2,1)}, bf16[128,512]{1,0:T(8,128)(2,1)S(1)}, u32[]{:S(2)}) copy-start(bf16[128,512]{1,0:T(8,128)(2,1)S(1)} %collective-permute-done.4) | copy-start | bytes 393220
  58.1 8.2 %collective-permute-start.5 = (bf16[128,512]{1,0:T(8,128)(2,1)S(1)}, bf16[128,512]{1,0:T(8,128)(2,1)S(1)}, u32[]{:S(2)}, u32[]{:S(2)}) collective-permute-start(bf16[128,512]{1,0:T(8,128)(2,1)S(1)} %collective-permute-done.4), channel_id=1, source_target_pairs={{0,2},{2,4},{4,6},{6,8},{8,10},{10,12},{12,14},{14,16},{16,18},{18... | collective-permute-start | bytes 393224 | tf_op jit(solution)/shard_map/ppermute | solution.py:77
  65.5 14.5 %copy-start.3 = (bf16[128,512]{1,0:T(8,128)(2,1)}, bf16[128,512]{1,0:T(8,128)(2,1)S(1)}, u32[]{:S(2)}) copy-start(bf16[128,512]{1,0:T(8,128)(2,1)S(1)} %collective-permute-done.11) | copy-start | bytes 393220
  65.5 14.7 %collective-permute-start.12 = (bf16[128,512]{1,0:T(8,128)(2,1)S(1)}, bf16[128,512]{1,0:T(8,128)(2,1)S(1)}, u32[]{:S(2)}, u32[]{:S(2)}) collective-permute-start(bf16[128,512]{1,0:T(8,128)(2,1)S(1)} %collective-permute-done.11), channel_id=1, source_target_pairs={{2,0},{4,2},{6,4},{8,6},{10,8},{12,10},{14,12},{16,14},{18,16},{20... | collective-permute-start | bytes 393224 | tf_op jit(solution)/shard_map/ppermute | solution.py:80
  66.4 13.6 %copy-start.7 = (bf16[128,512]{1,0:T(8,128)(2,1)}, bf16[128,512]{1,0:T(8,128)(2,1)S(1)}, u32[]{:S(2)}) copy-start(bf16[128,512]{1,0:T(8,128)(2,1)S(1)} %collective-permute-done.5) | copy-start | bytes 393220
  66.4 13.9 %collective-permute-start.6 = (bf16[128,512]{1,0:T(8,128)(2,1)S(1)}, bf16[128,512]{1,0:T(8,128)(2,1)S(1)}, u32[]{:S(2)}, u32[]{:S(2)}) collective-permute-start(bf16[128,512]{1,0:T(8,128)(2,1)S(1)} %collective-permute-done.5), channel_id=1, source_target_pairs={{0,2},{2,4},{4,6},{6,8},{8,10},{10,12},{12,14},{14,16},{16,18},{18... | collective-permute-start | bytes 393224 | tf_op jit(solution)/shard_map/ppermute | solution.py:77
  80.2 8.1 %collective-permute-start.13 = (bf16[128,512]{1,0:T(8,128)(2,1)S(1)}, bf16[128,512]{1,0:T(8,128)(2,1)S(1)}, u32[]{:S(2)}, u32[]{:S(2)}) collective-permute-start(bf16[128,512]{1,0:T(8,128)(2,1)S(1)} %collective-permute-done.12), channel_id=1, source_target_pairs={{2,0},{4,2},{6,4},{8,6},{10,8},{12,10},{14,12},{16,14},{18,16},{20... | collective-permute-start | bytes 393224 | tf_op jit(solution)/shard_map/ppermute | solution.py:80
  80.3 8.0 %collective-permute-start.7 = (bf16[128,512]{1,0:T(8,128)(2,1)S(1)}, bf16[128,512]{1,0:T(8,128)(2,1)S(1)}, u32[]{:S(2)}, u32[]{:S(2)}) collective-permute-start(bf16[128,512]{1,0:T(8,128)(2,1)S(1)} %collective-permute-done.6), channel_id=1, source_target_pairs={{0,2},{2,4},{4,6},{6,8},{8,10},{10,12},{12,14},{14,16},{16,18},{18... | collective-permute-start | bytes 393224 | tf_op jit(solution)/shard_map/ppermute | solution.py:77
  85.5 2.9 %copy-start.6 = (bf16[128,512]{1,0:T(8,128)(2,1)S(1)}, bf16[128,512]{1,0:T(8,128)(2,1)}, u32[]{:S(2)}) copy-start(bf16[128,512]{1,0:T(8,128)(2,1)} %copy-done.5) | copy-start | bytes 393220
  88.3 6.6 %collective-permute-start.14 = (bf16[128,512]{1,0:T(8,128)(2,1)S(1)}, bf16[128,512]{1,0:T(8,128)(2,1)S(1)}, u32[]{:S(2)}, u32[]{:S(2)}) collective-permute-start(bf16[128,512]{1,0:T(8,128)(2,1)S(1)} %collective-permute-done.13), channel_id=1, source_target_pairs={{2,0},{4,2},{6,4},{8,6},{10,8},{12,10},{14,12},{16,14},{18,16},{20... | collective-permute-start | bytes 393224 | tf_op jit(solution)/shard_map/ppermute | solution.py:80
  123.3 18.5 %copy-start.2 = (bf16[2048,1,128]{2,1,0:T(2,128)(2,1)S(1)}, bf16[2048,1,128]{2,1,0:T(2,128)(2,1)}, u32[]{:S(2)}) copy-start(bf16[2048,1,128]{2,1,0:T(2,128)(2,1)} %get-tuple-element.1018) | copy-start | bytes 1572868
  141.9 18.5 %copy-start.1 = (bf16[2048,1,128]{2,1,0:T(2,128)(2,1)S(1)}, bf16[2048,1,128]{2,1,0:T(2,128)(2,1)}, u32[]{:S(2)}) copy-start(bf16[2048,1,128]{2,1,0:T(2,128)(2,1)} %get-tuple-element.1019) | copy-start | bytes 1572868
  (2 other events, 5.3 us)
Sparse Core Ops, SparseCore 0:
  8.9 22.2 all-gather.2
  65.6 50.8 all-gather.4
